TPU v7x, 128 devices: a whole 4x4x4 slice. The times are simulated.
128 devices in a mesh: grp: 4 (over y), fsdp: 32 (over x, z, core).
Axes of the slice: x: 4, y: 4, z: 4, core: 2. Of those that a mesh axis runs over, the one named last changes fastest.
Arguments:
- hidden: bfloat16 [256, 257, 1024], P(('grp', 'fsdp')), may hold values from -6 to 6
- ln1_gain: float32 [1024], replicated, may hold values from 0.25 to 1.75
- w_qkv: bfloat16 [1024, 3072], P('fsdp'), may hold values from -0.1875 to 0.1875
- w_out: bfloat16 [1024, 1024], P('fsdp'), may hold values from -0.1875 to 0.1875
- ln2_gain: float32 [1024], replicated, may hold values from 0.25 to 1.75
- w_up: bfloat16 [1024, 4096], P('fsdp'), may hold values from -0.1875 to 0.1875
- w_down: bfloat16 [4096, 1024], P('fsdp'), may hold values from -0.09375 to 0.09375
- post_gain: float32 [1024], replicated, may hold values from 0.25 to 1.75
- w_proj: bfloat16 [1024, 256], replicated, may hold values from -0.1875 to 0.1875
- table: float32 [128, 2048, 256], P(('grp', 'fsdp')), may hold values from -6 to 6
- accum: float32 [128, 2048, 256], P(('grp', 'fsdp')), may hold values from 0.1 to 4
- place: int32 [128], replicated, may hold values from 0 to 127, each once
- lookup_table: int32 [16384, 1], P(('grp', 'fsdp')), may hold values from 0 to 127; in each aligned block of 128 rows (0 to 127, 128 to 255, ...) at most 2 rows name the same one
- lookup_row: int32 [16384], P(('grp', 'fsdp')), may hold values from 0 to 2047
Outputs:
- table_new: float32 [128, 2048, 256], P(('grp', 'fsdp'))
- accum_new: float32 [128, 2048, 256], P(('grp', 'fsdp'))
- content_grad: float32 [256, 256], P(('grp', 'fsdp'))
- proj_grad: float32 [1024, 256], P(('grp', 'fsdp'))
Inputs may be any that keep to these rules, and one draw needn't show every extreme that they name: `lookup_table`: within the lookups of one device (aligned blocks of 128), no table is named more than 2 times, a bound that some block reaches. `place`: every device holds exactly one table.
All inputs are finite; a program needn't handle non-finite values.
Results may differ from a plain program's by a relative error of at most 0.0044.
Values may be sent and summed in bfloat16 or wider, within the bound.
A program may use at most 192 MiB of HBM per device.

v0:
```python
import math
import jax
import jax.numpy as jnp
from jax import lax
from jax.sharding import Mesh
from jax.sharding import PartitionSpec as P

HEADS = 16
LOOK_IMG = 64
FSDP = ("fsdp_0", "fsdp_1", "fsdp_2")
GRP_FSDP = ("grp", "fsdp_0", "fsdp_1", "fsdp_2")
epsilon = 1e-06
learn_rate = 0.5


def sent_together(arrays, axis, dim, along):
    widths = [a.shape[along] for a in arrays]
    both = jnp.concatenate(arrays, axis=along)
    out = lax.all_gather(both, axis, axis=dim, tiled=True)
    return tuple(jnp.split(out, [sum(widths[:k]) for k in range(1, len(widths))], axis=along))


def in_blocks(array, dim, devices):
    shape = array.shape
    tiles = array.reshape(*shape[:dim], devices, shape[dim] // devices, *shape[dim + 1 :])
    return jnp.moveaxis(tiles, dim, 0)


def laid_out(tiles, dim):
    tiles = jnp.moveaxis(tiles, 0, dim)
    shape = tiles.shape
    return tiles.reshape(*shape[:dim], shape[dim] * shape[dim + 1], *shape[dim + 2 :])


def turned_blocks(tiles, axes, sequence):
    shape = [lax.axis_size(a) for a in axes]
    tiles = tiles.reshape(*shape, *tiles.shape[1:])
    for k in sequence:
        tiles = lax.all_to_all(tiles, axes[k], split_axis=k, concat_axis=k, tiled=True)
    return tiles.reshape(-1, *tiles.shape[len(axes) :])


def core_and_chips(array, groups, sequence, split_dim, concat_dim):
    devices = lax.axis_size(groups[0]) * lax.axis_size(groups[1])
    tiles = in_blocks(array, split_dim, devices)
    return laid_out(turned_blocks(tiles, groups, sequence), concat_dim)


def layer_norm(values, gain):
    center = jnp.mean(values, axis=-1, keepdims=True)
    shifted = values - center
    spread = jnp.mean(shifted * shifted, axis=-1, keepdims=True)
    return shifted * lax.rsqrt(spread + epsilon) * gain


def attend(qkv, images, seq, width):
    head_dim = width // HEADS
    parts = qkv.reshape(images, seq, 3, HEADS, head_dim)
    scores = jnp.einsum(
        "bqhd,bkhd->bhqk", parts[:, :, 0], parts[:, :, 1], preferred_element_type=jnp.float32
    ) / math.sqrt(head_dim)
    probs = jax.nn.softmax(scores, axis=-1).astype(jnp.bfloat16)
    mixed = jnp.einsum("bhqk,bkhd->bqhd", probs, parts[:, :, 2], preferred_element_type=jnp.float32)
    return mixed.astype(jnp.bfloat16).reshape(images * seq, width)


def on_device(
    hidden,
    ln1_gain,
    w_qkv,
    w_out,
    ln2_gain,
    w_up,
    w_down,
    post_gain,
    w_proj,
    table,
    accum,
    place,
    lookup_table,
    lookup_row,
):
    images, seq, width = hidden.shape
    count = images * seq
    tokens = hidden.reshape(count, width)
    full_qkv, full_out, full_up, full_down = (
        *sent_together((w_qkv, w_out, w_up), FSDP, 0, 1),
        lax.all_gather(w_down, FSDP, axis=0, tiled=True),
    )
    normed = layer_norm(tokens.astype(jnp.float32), ln1_gain).astype(jnp.bfloat16)
    qkv = jnp.dot(normed, full_qkv, preferred_element_type=jnp.float32)
    mixed = attend(qkv.astype(jnp.bfloat16), images, seq, width)
    projected = jnp.dot(mixed, full_out, preferred_element_type=jnp.float32)
    resid = (tokens.astype(jnp.float32) + projected).astype(jnp.bfloat16)
    normed_two = layer_norm(resid.astype(jnp.float32), ln2_gain).astype(jnp.bfloat16)
    upward = jnp.dot(normed_two, full_up, preferred_element_type=jnp.float32)
    active = jax.nn.gelu(upward, approximate=False).astype(jnp.bfloat16)
    downward = jnp.dot(active, full_down, preferred_element_type=jnp.float32)
    final = resid.astype(jnp.float32) + downward
    posted = layer_norm(final, post_gain).reshape(images, seq, width)
    pooled = jnp.mean(posted, axis=1).astype(jnp.bfloat16)
    content = jnp.dot(pooled, w_proj, preferred_element_type=jnp.float32)
    scale = lax.rsqrt(jnp.mean(content * content, axis=-1, keepdims=True) + epsilon)
    unit = content * scale
    proj_width = unit.shape[1]
    local_table = table[0]
    n_devices = lax.axis_size(GRP_FSDP)
    tables_count = place.shape[0]
    table_ids = jnp.arange(tables_count, dtype=jnp.int32)
    look_dev = lookup_row.shape[0]
    slots = max(2, (2 * look_dev + n_devices - 1) // n_devices)
    owners = jnp.sum(jnp.where(lookup_table == table_ids[None, :], place[None, :], 0), axis=1)
    hits = (owners[:, None] == jnp.arange(n_devices, dtype=jnp.int32)[None, :]).astype(jnp.int32)
    earlier = jnp.cumsum(hits, axis=0) - hits
    position = jnp.sum(earlier * hits, axis=1)
    target = owners * slots + position
    spread_unit = jnp.repeat(unit, LOOK_IMG, axis=0)
    send_vec = jnp.zeros((n_devices * slots, proj_width), jnp.float32).at[target].set(spread_unit)
    send_rows = jnp.full((n_devices * slots,), -1, jnp.int32).at[target].set(lookup_row)
    got_vec, got_rows = (
        core_and_chips(
            send_vec.reshape(n_devices, slots, proj_width),
            (("grp", "fsdp_0", "fsdp_1"), "fsdp_2"),
            (1, 0),
            0,
            0,
        ),
        core_and_chips(
            send_rows.reshape(n_devices, slots),
            (("grp", "fsdp_0", "fsdp_1"), "fsdp_2"),
            (1, 0),
            0,
            0,
        ),
    )
    flat_rows = got_rows.reshape(-1)
    valid = flat_rows >= 0
    safe_rows = jnp.where(valid, flat_rows, 0)
    diff = jnp.where(valid[:, None], local_table[safe_rows] - got_vec.reshape(-1, proj_width), 0.0)
    grad_rows = jnp.zeros(local_table.shape, jnp.float32).at[safe_rows].add(diff)
    returned = lax.all_to_all(
        -diff.reshape(n_devices, slots, proj_width),
        GRP_FSDP,
        split_axis=0,
        concat_axis=0,
        tiled=True,
    )
    per_lookup = returned.reshape(-1, proj_width)[target]
    grad_unit = jnp.sum(per_lookup.reshape(images, LOOK_IMG, proj_width), axis=1)
    accum_new = accum[0] + grad_rows * grad_rows
    table_new = local_table - learn_rate * grad_rows / jnp.sqrt(accum_new)
    inner = jnp.mean(grad_unit * unit, axis=-1, keepdims=True)
    content_grad = scale * (grad_unit - unit * inner)
    share = width // n_devices
    every_grad = lax.all_gather(content_grad, GRP_FSDP, axis=0, tiled=True)
    my_columns = lax.all_to_all(
        pooled.reshape(images, n_devices, share), GRP_FSDP, split_axis=1, concat_axis=0, tiled=True
    )
    column_block = my_columns.reshape(-1, share).astype(jnp.float32)
    proj_grad = jnp.dot(
        column_block.T,
        every_grad,
        precision=lax.Precision.HIGHEST,
        preferred_element_type=jnp.float32,
    )
    return (table_new[None], accum_new[None], content_grad, proj_grad)


def solution(mesh):
    torus = Mesh(
        mesh.devices.reshape(mesh.shape["grp"], 4, 4, 2), ("grp", "fsdp_0", "fsdp_1", "fsdp_2")
    )
    in_specs = (
        P(GRP_FSDP, None, None),
        P(),
        P(FSDP, None),
        P(FSDP, None),
        P(),
        P(FSDP, None),
        P(FSDP, None),
        P(),
        P(),
        P(GRP_FSDP, None, None),
        P(GRP_FSDP, None, None),
        P(),
        P(GRP_FSDP, None),
        P(GRP_FSDP),
    )
    out_specs = (
        P(GRP_FSDP, None, None),
        P(GRP_FSDP, None, None),
        P(GRP_FSDP, None),
        P(GRP_FSDP, None),
    )
    return jax.shard_map(
        on_device, mesh=torus, in_specs=in_specs, out_specs=out_specs, check_vma=False
    )
```

profile of v0, /device:TPU:1, one launch (start us, length us, event | category | flops | bytes accessed | tf_op | source)
XLA Modules:
  0.0 299.2 jit_solution(8550466060743165538)
XLA Ops:
  12.7 4.7 %all_to_all.40 = s32[2,1,128]{2,1,0:T(1,128)S(1)} all-to-all(s32[2,1,128]{2,1,0:T(1,128)S(1)} %reshape.241), channel_id=1, replica_groups=mesh['grp'=4,'fsdp_0'=4,'fsdp_1'=4,'fsdp_2'=2] {'fsdp_2'}, dimensions={0} | all-to-all | bytes 2048 | tf_op jit(solution)/shard_map/all_to_all | solution.py:39
  19.4 11.5 %all-to-all-start.1 = ((s32[64,2,1,2]{3,1,2,0:T(2,128)}), s32[64,2,1,2]{3,1,2,0:T(2,128)S(1)}, u32[]{:S(2)}, u32[]{:S(2)}) async-start(s32[64,2,1,2]{3,1,2,0:T(2,128)} %copy.51), calls=%async_computation.1 | async-start | bytes 131072 | tf_op jit(solution)/shard_map/all_to_all | solution.py:39
  33.1 2.8 multiply_reduce_fusion.2
  40.3 47.6 %all-gather.4.cloned.1.call-done = bf16[1024,8192]{1,0:T(8,128)(2,1)} async-done(((bf16[32,8192]{1,0:T(8,128)(2,1)}), bf16[1024,8192]{1,0:T(8,128)(2,1)}) %all-gather.4.cloned.1.call-update) | async-done | bytes 16777232 | tf_op jit(solution)/shard_map/all_gather | solution.py:19
  87.9 8.8 %fusion.20 = bf16[514,3072]{1,0:T(8,128)(2,1)} fusion(bf16[1024,8192]{1,0:T(8,128)(2,1)} %all-gather.4.cloned.1.call-done, f32[514,1024]{1,0:T(8,128)} %reshape.190, f32[1024]{0:T(1024)S(1)} %copy-done.5, f32[514]{0:T(1024)S(1)} %rsqrt.37, f32[514]{0:T(1024)S(1)} %div.50), kind=kOutput, calls=%fused_computation.35 | convolution fusion | flops 3237492736 | bytes 11587600 | tf_op jit(solution)/shard_map/dot_general | solution.py:91
  96.7 8.7 %reshape.234 = bf16[2,257,3,16,64]{4,3,2,1,0:T(8,128)(2,1)} reshape(bf16[514,3072]{1,0:T(8,128)(2,1)} %fusion.20) | data formatting | bytes 6316032 | tf_op jit(solution)/shard_map/reshape | solution.py:58
  105.4 6.1 %fusion.107 = (bf16[2,257,1,16,64]{4,3,2,1,0:T(8,128)(2,1)S(1)}, bf16[2,257,1,16,64]{4,3,2,1,0:T(8,128)(2,1)}, bf16[2,257,1,16,64]{4,3,2,1,0:T(8,128)(2,1)}) fusion(bf16[2,257,3,16,64]{4,3,2,1,0:T(8,128)(2,1)} %reshape.234), kind=kLoop, calls=%fused_computation.139 | loop fusion | bytes 6316032 | tf_op jit(solution)/shard_map/slice | solution.py:63
  111.4 4.3 %copy.72 = bf16[2,257,1,16,64]{1,4,3,0,2:T(8,128)(2,1)} copy(bf16[2,257,1,16,64]{4,3,2,1,0:T(8,128)(2,1)} %get-tuple-element.5) | data formatting | bytes 2105344
  115.7 4.3 %copy.73 = bf16[2,257,1,16,64]{1,4,3,0,2:T(8,128)(2,1)} copy(bf16[2,257,1,16,64]{4,3,2,1,0:T(8,128)(2,1)} %get-tuple-element.6) | data formatting | bytes 2105344
  120.0 4.1 %copy.71 = bf16[2,257,1,16,64]{1,4,3,0,2:T(8,128)(2,1)} copy(bf16[2,257,1,16,64]{4,3,2,1,0:T(8,128)(2,1)S(1)} %get-tuple-element.4) | data formatting | bytes 2105344
  124.2 9.4 %fusion.41 = f32[2,16,257,257]{2,3,1,0:T(8,128)} fusion(bf16[2,257,1,16,64]{1,4,3,0,2:T(8,128)(2,1)} %copy.73, bf16[2,257,1,16,64]{1,4,3,0,2:T(8,128)(2,1)} %copy.72), kind=kOutput, calls=%fused_computation.55 | convolution fusion | flops 270536704 | bytes 10559616 | tf_op jit(solution)/shard_map/bqhd,bkhd->bhqk/dot_general | solution.py:59
  133.5 17.2 %fusion.108 = (f32[2,16,257]{2,1,0:T(8,128)S(1)}, f32[2,16,257,257]{2,3,1,0:T(8,128)}) fusion(f32[2,16,257,257]{2,3,1,0:T(8,128)} %fusion.41), kind=kOutput, calls=%fused_computation.140 | output fusion | flops 8454528 | bytes 16941440 | tf_op jit(solution)/shard_map/sub | solution.py:62
  150.7 6.4 %fusion.45 = bf16[2,257,16,64]{1,3,2,0:T(8,128)(2,1)S(1)} fusion(f32[2,16,257,257]{2,3,1,0:T(8,128)} %get-tuple-element.10, f32[2,16,257]{2,1,0:T(8,128)S(1)} %get-tuple-element.9, bf16[2,257,1,16,64]{1,4,3,0,2:T(8,128)(2,1)S(1)} %copy-done.2), kind=kOutput, calls=%fused_computation.59 | convolution fusion | flops 275290176 | bytes 10592512 | tf_op jit(solution)/shard_map/bhqk,bkhd->bqhd/dot_general | solution.py:63
  160.0 3.7 %convert_reduce_fusion = (f32[514]{0:T(1024)S(1)}, bf16[514,1024]{1,0:T(8,128)(2,1)S(1)}) fusion(f32[514,1024]{1,0:T(8,128)} %reshape.190, bf16[514,1024]{0,1:T(8,128)(2,1)S(1)} %reshape.184, bf16[1024,8192]{1,0:T(8,128)(2,1)} %all-gather.4.cloned.1.call-done), kind=kOutput, calls=%fused_computation.39 | convolution fusion | flops 1080040960 | bytes 6334472 | tf_op jit(solution)/shard_map/dot_general | solution.py:93
  164.1 26.2 %fusion.40.clone.4 = bf16[514,4096]{1,0:T(8,128)(2,1)} fusion(bf16[1024,8192]{1,0:T(8,128)(2,1)} %all-gather.4.cloned.1.call-done, bf16[514,1024]{1,0:T(8,128)(2,1)S(1)} %get-tuple-element.12, f32[1024]{0:T(1024)S(1)} %copy-done.6, f32[514]{0:T(1024)S(1)} %add_rsqrt_fusion.2, f32[514]{0:T(1024)S(1)} %broadcast_multiply_fusion.2), kind=kOutput, calls=%fused_computation.13.clone.clone.clone.clone.clone.clone.1 | convolution fusion | flops 4451223552 | bytes 13660176 | tf_op jit(solution)/shard_map/dot_general | solution.py:96
  190.3 8.7 %fusion.109 = (f32[514]{0:T(1024)S(1)}, f32[514,1024]{1,0:T(8,128)S(1)}) fusion(bf16[4096,1024]{1,0:T(8,128)(2,1)} %all-gather.6.cloned.1.call-done, bf16[514,1024]{1,0:T(8,128)(2,1)S(1)} %get-tuple-element.12, bf16[514,4096]{1,0:T(8,128)(2,1)} %fusion.40.clone.4), kind=kOutput, calls=%fused_computation.141 | convolution fusion | flops 4313323008 | bytes 15759368 | tf_op jit(solution)/shard_map/dot_general | solution.py:98
  204.8 4.0 %all_to_all.41 = f32[64,2,1,2,256]{4,3,0,2,1:T(2,128)S(1)} all-to-all(f32[64,2,1,2,256]{4,3,0,2,1:T(2,128)S(1)} %copy.62), channel_id=1, replica_groups=mesh['grp'=4,'fsdp_0'=4,'fsdp_1'=4,'fsdp_2'=2] {'fsdp_2'}, dimensions={1} | all-to-all | bytes 524288 | tf_op jit(solution)/shard_map/all_to_all | solution.py:39
  209.5 8.1 %all-to-all-start.3 = ((f32[64,2,1,2,256]{4,3,1,2,0:T(2,128)}), f32[64,2,1,2,256]{4,3,1,2,0:T(2,128)S(1)}, u32[]{:S(2)}, u32[]{:S(2)}) async-start(f32[64,2,1,2,256]{4,3,1,2,0:T(2,128)} %copy.63), calls=%async_computation.3 | async-start | bytes 524288 | tf_op jit(solution)/shard_map/all_to_all | solution.py:39
  221.2 6.4 %all-to-all-done.3 = f32[64,2,1,2,256]{4,3,1,2,0:T(2,128)S(1)} async-done(((f32[64,2,1,2,256]{4,3,1,2,0:T(2,128)}), f32[64,2,1,2,256]{4,3,1,2,0:T(2,128)S(1)}, u32[]{:S(2)}, u32[]{:S(2)}) %all-to-all-start.3) | async-done | bytes 262176 | tf_op jit(solution)/shard_map/all_to_all | solution.py:39
  228.5 5.1 %all-to-all-start.4 = ((f32[128,2,256]{2,1,0:T(2,128)}), f32[128,2,256]{2,1,0:T(2,128)S(1)}, u32[]{:S(2)}, u32[]{:S(2)}) async-start(f32[128,2,256]{2,1,0:T(2,128)} %fusion.65), calls=%async_computation.4 | async-start | bytes 524288 | tf_op jit(solution)/shard_map/all_to_all | solution.py:141
  234.5 3.9 %scatter_custom_fusion.2 = f32[2048,256]{1,0:T(8,128)} fusion(s32[256]{0:T(256)S(1)} %bitcast.73, f32[]{:T(128)} %constant.41.clone.1, f32[256,256]{1,0:T(8,128)S(1)} %gather_fusion, f32[256,256]{1,0:T(8,128)} %reshape_reshape_reshape.17, pred[256]{0:T(512)(128)(4,1)S(1)} %ge.24), kind=kCustom, calls=%fused_computation.67 | custom fusion | flops 196608 | bytes 2622976 | tf_op jit(solution)/shard_map/scatter-add | solution.py:140
  238.3 4.7 %fusion.63 = (f32[1,2048,256]{2,1,0:T(8,128)}, f32[1,2048,256]{2,1,0:T(8,128)}) fusion(f32[2048,256]{1,0:T(8,128)} %scatter_custom_fusion.2, f32[1,2048,256]{2,1,0:T(8,128)} %param.24, f32[1,2048,256]{2,1,0:T(8,128)S(1)} %copy-done.1), kind=kLoop, calls=%fused_computation.69 | loop fusion | flops 2621440 | bytes 10485760 | tf_op jit(solution)/shard_map/broadcast_in_dim | solution.py:166
  244.6 8.3 %all-to-all-start.5 = ((bf16[2,128,8]{2,0,1:T(2,128)(2,1)}), bf16[2,128,8]{2,0,1:T(2,128)(2,1)S(1)}, u32[]{:S(2)}, u32[]{:S(2)}) async-start(bf16[2,128,8]{2,0,1:T(2,128)(2,1)} %copy.66), calls=%async_computation.5 | async-start | bytes 131072 | tf_op jit(solution)/shard_map/all_to_all | solution.py:156
  254.1 37.0 %all-gather = f32[128,2,256]{2,1,0:T(2,128)S(1)} all-gather(f32[1,2,256]{2,1,0:T(2,128)S(1)} %bitcast.69), channel_id=1, replica_groups=mesh['grp'=4,'fsdp_0'=4,'fsdp_1'=4,'fsdp_2'=2] {'grp','fsdp_0','fsdp_1',..., dimensions={0}, use_global_device_ids=true | all-gather | bytes 264192 | tf_op jit(solution)/shard_map/all_gather | solution.py:155
  (86 shorter events, 32.8 us)
Async XLA Ops:
  7.2 195.9 %copy-start = (bf16[1024,256]{1,0:T(8,128)(2,1)S(1)}, bf16[1024,256]{1,0:T(8,128)(2,1)}, u32[]{:S(2)}) copy-start(bf16[1024,256]{1,0:T(8,128)(2,1)} %param.22) | copy-start | bytes 1572868
  7.2 80.7 %all-gather.4.cloned.1.call-start = ((), (), s32[]{:S(2)}) async-start(), calls=%async_computation.6 | async-start | bytes 17301504 | tf_op jit(solution)/shard_map/all_gather | solution.py:19
  9.1 78.7 %copy-start.5 = (f32[1024]{0:T(1024)S(1)}, f32[1024]{0:T(1024)}, u32[]{:S(2)}) copy-start(f32[1024]{0:T(1024)} %param.15) | copy-start | bytes 12292
  9.2 181.1 %all-gather.6.cloned.1.call-start = ((), (), s32[]{:S(2)}) async-start(), calls=%async_computation.7 | async-start | bytes 8650752 | tf_op jit(solution)/shard_map/all_gather | solution.py:88
  19.4 20.5 %all-to-all-start.1 = ((s32[64,2,1,2]{3,1,2,0:T(2,128)}), s32[64,2,1,2]{3,1,2,0:T(2,128)S(1)}, u32[]{:S(2)}, u32[]{:S(2)}) async-start(s32[64,2,1,2]{3,1,2,0:T(2,128)} %copy.51), calls=%async_computation.1 | async-start | bytes 131072 | tf_op jit(solution)/shard_map/all_to_all | solution.py:39
  133.5 17.2 %copy-start.2 = (bf16[2,257,1,16,64]{1,4,3,0,2:T(8,128)(2,1)S(1)}, bf16[2,257,1,16,64]{1,4,3,0,2:T(8,128)(2,1)}, u32[]{:S(2)}) copy-start(bf16[2,257,1,16,64]{1,4,3,0,2:T(8,128)(2,1)} %copy.71) | copy-start | bytes 3158020
  160.0 4.1 %copy-start.6 = (f32[1024]{0:T(1024)S(1)}, f32[1024]{0:T(1024)}, u32[]{:S(2)}) copy-start(f32[1024]{0:T(1024)} %param.18) | copy-start | bytes 12292
  190.3 9.1 %copy-start.4 = (f32[1024]{0:T(1024)S(1)}, f32[1024]{0:T(1024)}, u32[]{:S(2)}) copy-start(f32[1024]{0:T(1024)} %param.21) | copy-start | bytes 12292
  203.0 35.3 %copy-start.1 = (f32[1,2048,256]{2,1,0:T(8,128)S(1)}, f32[1,2048,256]{2,1,0:T(8,128)}, u32[]{:S(2)}) copy-start(f32[1,2048,256]{2,1,0:T(8,128)} %param.23) | copy-start | bytes 6291460
  209.5 18.0 %all-to-all-start.3 = ((f32[64,2,1,2,256]{4,3,1,2,0:T(2,128)}), f32[64,2,1,2,256]{4,3,1,2,0:T(2,128)S(1)}, u32[]{:S(2)}, u32[]{:S(2)}) async-start(f32[64,2,1,2,256]{4,3,1,2,0:T(2,128)} %copy.63), calls=%async_computation.3 | async-start | bytes 524288 | tf_op jit(solution)/shard_map/all_to_all | solution.py:39
  228.5 16.0 %all-to-all-start.4 = ((f32[128,2,256]{2,1,0:T(2,128)}), f32[128,2,256]{2,1,0:T(2,128)S(1)}, u32[]{:S(2)}, u32[]{:S(2)}) async-start(f32[128,2,256]{2,1,0:T(2,128)} %fusion.65), calls=%async_computation.4 | async-start | bytes 524288 | tf_op jit(solution)/shard_map/all_to_all | solution.py:141
  244.6 46.8 %all-to-all-start.5 = ((bf16[2,128,8]{2,0,1:T(2,128)(2,1)}), bf16[2,128,8]{2,0,1:T(2,128)(2,1)S(1)}, u32[]{:S(2)}, u32[]{:S(2)}) async-start(bf16[2,128,8]{2,0,1:T(2,128)(2,1)} %copy.66), calls=%async_computation.5 | async-start | bytes 131072 | tf_op jit(solution)/shard_map/all_to_all | solution.py:156
  254.1 38.0 %copy-start.3 = (f32[2,256]{1,0:T(2,128)}, f32[2,256]{1,0:T(2,128)S(1)}, u32[]{:S(2)}) copy-start(f32[2,256]{1,0:T(2,128)S(1)} %subtract_multiply_fusion) | copy-start | bytes 6148
Sparse Core Ops, SparseCore 0:
  10.8 77.0 all-gather.3
  90.1 52.2 all-gather.5
where the time goes:
time: 303 us; the launch traced here: 299 us
  matrix products  64.2 us (21%)
  waiting for transfers between devices  56.6 us (19%)
  local copies, waits for them, and re-layouts  46.3 us (15%)
  blocking collectives  45.8 us (15%)
  other arithmetic  38.7 us (13%)
  starting transfers between devices  33.1 us (11%)
  between operations  14.6 us (5%)
    all_gather x1, waiting for transfers between devices, sent_together(): out = lax.all_gather(both, axis, axis=dim, tiled=True)  47.6 us
    all_gather x1, blocking collectives, on_device(): every_grad = lax.all_gather(content_grad, GRP_FSDP, axis=0, tiled=True)  37 us
    dot_general x1, matrix products, on_device(): upward = jnp.dot(normed_two, full_up, preferred_element_type=jnp.float32)  26.2 us
    all_to_all x2, starting transfers between devices, turned_blocks(): lax.all_to_all(tiles, axes[k], split_axis=k, concat_axis=k, tiled=True)  19.6 us
    sub x1, other arithmetic, attend(): probs = jax.nn.softmax(scores, axis=-1).astype(jnp.bfloat16)  17.2 us
    unnamed x22, local copies, waits for them, and re-layouts  13.3 us
    dot_general x1, matrix products, attend(): jnp.einsum('bqhd,bkhd->bhqk', parts[:, :, 0], parts[:, :, 1], preferred_e...  9.35 us
    dot_general x1, matrix products, on_device(): qkv = jnp.dot(normed, full_qkv, preferred_element_type=jnp.float32)  8.78 us
  transfers between devices with their start and end apart: 6, of which 4 were waited for; matrix products, arithmetic and copies ran while one was open for 44% of the time, Pallas kernels for 0%

commit v1 on v0

--- a/solution.py
+++ b/solution.py
@@ -152,7 +152,9 @@
     inner = jnp.mean(grad_unit * unit, axis=-1, keepdims=True)
     content_grad = scale * (grad_unit - unit * inner)
     share = width // n_devices
-    every_grad = lax.all_gather(content_grad, GRP_FSDP, axis=0, tiled=True)
+    every_grad = jnp.concatenate(
+        lax.all_to_all(jnp.stack([content_grad] * lax.axis_size(GRP_FSDP)), GRP_FSDP, 0, 0), axis=0
+    )
     my_columns = lax.all_to_all(
         pooled.reshape(images, n_devices, share), GRP_FSDP, split_axis=1, concat_axis=0, tiled=True
     )

time: 303 us -> 290 us (0.957)
  blocking collectives: 45.8 us -> 8.88 us
  waiting for transfers between devices: 56.6 us -> 75.8 us
    all_gather x1 -> x0, blocking collectives: 37 us -> none  [on_device(): every_grad = lax.all_gather(content_grad, GRP_FSDP, axis=0, tiled=True)]
    all_to_all x1, waiting for transfers between devices: 1.5 us -> 10.7 us  [on_device(): lax.all_to_all(-diff.reshape(n_devices, slots, proj_width), GRP_FSDP, spl...]
    all_to_all x0 -> x1, waiting for transfers between devices: none -> 4.56 us  [on_device(): lax.all_to_all(jnp.stack([content_grad] * lax.axis_size(GRP_FSDP)), GRP_F...]
    all_to_all x1, waiting for transfers between devices: 0.01 us -> 4.52 us  [on_device(): lax.all_to_all(pooled.reshape(images, n_devices, share), GRP_FSDP, split_...]
    all_to_all x0 -> x1, starting transfers between devices: none -> 4.44 us  [on_device(): lax.all_to_all(jnp.stack([content_grad] * lax.axis_size(GRP_FSDP)), GRP_F...]
    unnamed x22 -> x25, local copies, waits for them, and re-layouts: 13.3 us -> 13.2 us
  transfers between devices with their start and end apart: 6 -> 7, of which waited for: 4 -> 6; matrix products, arithmetic and copies ran while one was open for 44% -> 45% of each run, Pallas kernels for 0% -> 0%
where the time goes in v1:
time: 290 us; the launch traced here: 287 us
  waiting for transfers between devices  75.8 us (26%)
  matrix products  64.2 us (22%)
  local copies, waits for them, and re-layouts  48.8 us (17%)
  other arithmetic  38.7 us (13%)
  starting transfers between devices  35.5 us (12%)
  between operations  14.6 us (5%)
  blocking collectives  8.88 us (3%)
    all_gather x1, waiting for transfers between devices, sent_together(): out = lax.all_gather(both, axis, axis=dim, tiled=True)  47.8 us
    dot_general x1, matrix products, on_device(): upward = jnp.dot(normed_two, full_up, preferred_element_type=jnp.float32)  26.2 us
    all_to_all x2, starting transfers between devices, turned_blocks(): lax.all_to_all(tiles, axes[k], split_axis=k, concat_axis=k, tiled=True)  19.6 us
    sub x1, other arithmetic, attend(): probs = jax.nn.softmax(scores, axis=-1).astype(jnp.bfloat16)  17.2 us
    unnamed x25, local copies, waits for them, and re-layouts  13.2 us
    all_to_all x1, waiting for transfers between devices, on_device(): lax.all_to_all(-diff.reshape(n_devices, slots, proj_width), GRP_FSDP, spl...  10.7 us
    dot_general x1, matrix products, attend(): jnp.einsum('bqhd,bkhd->bhqk', parts[:, :, 0], parts[:, :, 1], preferred_e...  9.35 us
    all_to_all x2, blocking collectives, turned_blocks(): lax.all_to_all(tiles, axes[k], split_axis=k, concat_axis=k, tiled=True)  8.88 us
  transfers between devices with their start and end apart: 7, of which 6 were waited for; matrix products, arithmetic and copies ran while one was open for 45% of the time, Pallas kernels for 0%

profile of v1, /device:TPU:1, one launch (start us, length us, event | category | flops | bytes accessed | tf_op | source)
XLA Modules:
  0.0 286.5 jit_solution(7880709803776496600)
XLA Ops:
  12.7 4.7 %all_to_all.45 = s32[2,1,128]{2,1,0:T(1,128)S(1)} all-to-all(s32[2,1,128]{2,1,0:T(1,128)S(1)} %reshape.245), channel_id=1, replica_groups=mesh['grp'=4,'fsdp_0'=4,'fsdp_1'=4,'fsdp_2'=2] {'fsdp_2'}, dimensions={0} | all-to-all | bytes 2048 | tf_op jit(solution)/shard_map/all_to_all | solution.py:39
  19.4 11.5 %all-to-all-start.1 = ((s32[64,2,1,2]{3,1,2,0:T(2,128)}), s32[64,2,1,2]{3,1,2,0:T(2,128)S(1)}, u32[]{:S(2)}, u32[]{:S(2)}) async-start(s32[64,2,1,2]{3,1,2,0:T(2,128)} %copy.51), calls=%async_computation.1 | async-start | bytes 131072 | tf_op jit(solution)/shard_map/all_to_all | solution.py:39
  40.1 47.8 %all-gather.3.cloned.1.call-done = bf16[1024,8192]{1,0:T(8,128)(2,1)} async-done(((bf16[32,8192]{1,0:T(8,128)(2,1)}), bf16[1024,8192]{1,0:T(8,128)(2,1)}) %all-gather.3.cloned.1.call-update) | async-done | bytes 16777232 | tf_op jit(solution)/shard_map/all_gather | solution.py:19
  87.9 8.8 %fusion.20 = bf16[514,3072]{1,0:T(8,128)(2,1)} fusion(bf16[1024,8192]{1,0:T(8,128)(2,1)} %all-gather.3.cloned.1.call-done, f32[514,1024]{1,0:T(8,128)} %reshape.196, f32[1024]{0:T(1024)S(1)} %copy-done.7, f32[514]{0:T(1024)S(1)} %rsqrt.37, f32[514]{0:T(1024)S(1)} %div.50), kind=kOutput, calls=%fused_computation.35 | convolution fusion | flops 3237492736 | bytes 11587600 | tf_op jit(solution)/shard_map/dot_general | solution.py:91
  96.7 8.7 %reshape.238 = bf16[2,257,3,16,64]{4,3,2,1,0:T(8,128)(2,1)} reshape(bf16[514,3072]{1,0:T(8,128)(2,1)} %fusion.20) | data formatting | bytes 6316032 | tf_op jit(solution)/shard_map/reshape | solution.py:58
  105.4 6.1 %fusion.107 = (bf16[2,257,1,16,64]{4,3,2,1,0:T(8,128)(2,1)S(1)}, bf16[2,257,1,16,64]{4,3,2,1,0:T(8,128)(2,1)}, bf16[2,257,1,16,64]{4,3,2,1,0:T(8,128)(2,1)}) fusion(bf16[2,257,3,16,64]{4,3,2,1,0:T(8,128)(2,1)} %reshape.238), kind=kLoop, calls=%fused_computation.139 | loop fusion | bytes 6316032 | tf_op jit(solution)/shard_map/slice | solution.py:63
  111.4 4.3 %copy.72 = bf16[2,257,1,16,64]{1,4,3,0,2:T(8,128)(2,1)} copy(bf16[2,257,1,16,64]{4,3,2,1,0:T(8,128)(2,1)} %get-tuple-element.5) | data formatting | bytes 2105344
  115.7 4.3 %copy.73 = bf16[2,257,1,16,64]{1,4,3,0,2:T(8,128)(2,1)} copy(bf16[2,257,1,16,64]{4,3,2,1,0:T(8,128)(2,1)} %get-tuple-element.6) | data formatting | bytes 2105344
  120.0 4.1 %copy.71 = bf16[2,257,1,16,64]{1,4,3,0,2:T(8,128)(2,1)} copy(bf16[2,257,1,16,64]{4,3,2,1,0:T(8,128)(2,1)S(1)} %get-tuple-element.4) | data formatting | bytes 2105344
  124.2 9.4 %fusion.41 = f32[2,16,257,257]{2,3,1,0:T(8,128)} fusion(bf16[2,257,1,16,64]{1,4,3,0,2:T(8,128)(2,1)} %copy.73, bf16[2,257,1,16,64]{1,4,3,0,2:T(8,128)(2,1)} %copy.72), kind=kOutput, calls=%fused_computation.55 | convolution fusion | flops 270536704 | bytes 10559616 | tf_op jit(solution)/shard_map/bqhd,bkhd->bhqk/dot_general | solution.py:59
  133.5 17.2 %fusion.108 = (f32[2,16,257]{2,1,0:T(8,128)S(1)}, f32[2,16,257,257]{2,3,1,0:T(8,128)}) fusion(f32[2,16,257,257]{2,3,1,0:T(8,128)} %fusion.41), kind=kOutput, calls=%fused_computation.140 | output fusion | flops 8454528 | bytes 16941440 | tf_op jit(solution)/shard_map/sub | solution.py:62
  150.7 6.4 %fusion.45 = bf16[2,257,16,64]{1,3,2,0:T(8,128)(2,1)S(1)} fusion(f32[2,16,257,257]{2,3,1,0:T(8,128)} %get-tuple-element.10, f32[2,16,257]{2,1,0:T(8,128)S(1)} %get-tuple-element.9, bf16[2,257,1,16,64]{1,4,3,0,2:T(8,128)(2,1)S(1)} %copy-done.2), kind=kOutput, calls=%fused_computation.59 | convolution fusion | flops 275290176 | bytes 10592512 | tf_op jit(solution)/shard_map/bhqk,bkhd->bqhd/dot_general | solution.py:63
  164.1 26.2 %fusion.40.clone.4 = bf16[514,4096]{1,0:T(8,128)(2,1)} fusion(bf16[1024,8192]{1,0:T(8,128)(2,1)} %all-gather.3.cloned.1.call-done, bf16[514,1024]{1,0:T(8,128)(2,1)S(1)} %get-tuple-element.12, f32[1024]{0:T(1024)S(1)} %copy-done.8, f32[514]{0:T(1024)S(1)} %add_rsqrt_fusion.2, f32[514]{0:T(1024)S(1)} %broadcast_multiply_fusion.2), kind=kOutput, calls=%fused_computation.13.clone.clone.clone.clone.clone.clone.1 | convolution fusion | flops 4451223552 | bytes 13660176 | tf_op jit(solution)/shard_map/dot_general | solution.py:96
  190.3 8.7 %fusion.109 = (f32[514]{0:T(1024)S(1)}, f32[514,1024]{1,0:T(8,128)S(1)}) fusion(bf16[4096,1024]{1,0:T(8,128)(2,1)} %all-gather.5.cloned.1.call-done, bf16[514,1024]{1,0:T(8,128)(2,1)S(1)} %get-tuple-element.12, bf16[514,4096]{1,0:T(8,128)(2,1)} %fusion.40.clone.4), kind=kOutput, calls=%fused_computation.141 | convolution fusion | flops 4313323008 | bytes 15759368 | tf_op jit(solution)/shard_map/dot_general | solution.py:98
  204.8 4.1 %all_to_all.46 = f32[64,2,1,2,256]{4,3,0,2,1:T(2,128)S(1)} all-to-all(f32[64,2,1,2,256]{4,3,0,2,1:T(2,128)S(1)} %copy.62), channel_id=1, replica_groups=mesh['grp'=4,'fsdp_0'=4,'fsdp_1'=4,'fsdp_2'=2] {'fsdp_2'}, dimensions={1} | all-to-all | bytes 524288 | tf_op jit(solution)/shard_map/all_to_all | solution.py:39
  209.7 8.1 %all-to-all-start.3 = ((f32[64,2,1,2,256]{4,3,1,2,0:T(2,128)}), f32[64,2,1,2,256]{4,3,1,2,0:T(2,128)S(1)}, u32[]{:S(2)}, u32[]{:S(2)}) async-start(f32[64,2,1,2,256]{4,3,1,2,0:T(2,128)} %copy.63), calls=%async_computation.3 | async-start | bytes 524288 | tf_op jit(solution)/shard_map/all_to_all | solution.py:39
  220.6 7.1 %all-to-all-done.3 = f32[64,2,1,2,256]{4,3,1,2,0:T(2,128)S(1)} async-done(((f32[64,2,1,2,256]{4,3,1,2,0:T(2,128)}), f32[64,2,1,2,256]{4,3,1,2,0:T(2,128)S(1)}, u32[]{:S(2)}, u32[]{:S(2)}) %all-to-all-start.3) | async-done | bytes 262176 | tf_op jit(solution)/shard_map/all_to_all | solution.py:39
  228.7 6.1 %all-to-all-start.4 = ((f32[128,2,256]{2,1,0:T(2,128)}), f32[128,2,256]{2,1,0:T(2,128)}, u32[]{:S(2)}, u32[]{:S(2)}) async-start(f32[128,2,256]{2,1,0:T(2,128)} %fusion.65), calls=%async_computation.4 | async-start | bytes 524288 | tf_op jit(solution)/shard_map/all_to_all | solution.py:141
  234.7 10.7 %all-to-all-done.4 = f32[128,2,256]{2,1,0:T(2,128)} async-done(((f32[128,2,256]{2,1,0:T(2,128)}), f32[128,2,256]{2,1,0:T(2,128)}, u32[]{:S(2)}, u32[]{:S(2)}) %all-to-all-start.4) | async-done | bytes 262176 | tf_op jit(solution)/shard_map/all_to_all | solution.py:141
  248.4 4.4 %all-to-all-start.6 = ((f32[128,2,256]{2,1,0:T(2,128)}), f32[128,2,256]{2,1,0:T(2,128)S(1)}, u32[]{:S(2)}, u32[]{:S(2)}) async-start(f32[128,2,256]{2,1,0:T(2,128)} %stack.2), calls=%async_computation.6 | async-start | bytes 524288 | tf_op jit(solution)/shard_map/all_to_all | solution.py:156
  259.3 4.6 %all-to-all-done.6 = f32[128,2,256]{2,1,0:T(2,128)S(1)} async-done(((f32[128,2,256]{2,1,0:T(2,128)}), f32[128,2,256]{2,1,0:T(2,128)S(1)}, u32[]{:S(2)}, u32[]{:S(2)}) %all-to-all-start.6) | async-done | bytes 262176 | tf_op jit(solution)/shard_map/all_to_all | solution.py:156
  263.9 5.3 %all-to-all-start.5 = ((bf16[2,128,8]{2,0,1:T(2,128)(2,1)}), bf16[2,128,8]{2,0,1:T(2,128)(2,1)S(1)}, u32[]{:S(2)}, u32[]{:S(2)}) async-start(bf16[2,128,8]{2,0,1:T(2,128)(2,1)} %copy.66), calls=%async_computation.5 | async-start | bytes 131072 | tf_op jit(solution)/shard_map/all_to_all | solution.py:158
  269.2 4.7 %fusion.63 = (f32[1,2048,256]{2,1,0:T(8,128)}, f32[1,2048,256]{2,1,0:T(8,128)}) fusion(f32[2048,256]{1,0:T(8,128)} %scatter_custom_fusion.2, f32[1,2048,256]{2,1,0:T(8,128)} %param.24, f32[1,2048,256]{2,1,0:T(8,128)S(1)} %copy-done.1), kind=kLoop, calls=%fused_computation.69 | loop fusion | flops 2621440 | bytes 10485760 | tf_op jit(solution)/shard_map/broadcast_in_dim | solution.py:168
  274.1 4.5 %all-to-all-done.5 = bf16[2,128,8]{2,0,1:T(2,128)(2,1)S(1)} async-done(((bf16[2,128,8]{2,0,1:T(2,128)(2,1)}), bf16[2,128,8]{2,0,1:T(2,128)(2,1)S(1)}, u32[]{:S(2)}, u32[]{:S(2)}) %all-to-all-start.5) | async-done | bytes 4128 | tf_op jit(solution)/shard_map/all_to_all | solution.py:158
  (92 shorter events, 44.1 us)
Async XLA Ops:
  7.2 195.9 %copy-start = (bf16[1024,256]{1,0:T(8,128)(2,1)S(1)}, bf16[1024,256]{1,0:T(8,128)(2,1)}, u32[]{:S(2)}) copy-start(bf16[1024,256]{1,0:T(8,128)(2,1)} %param.22) | copy-start | bytes 1572868
  7.2 80.7 %all-gather.3.cloned.1.call-start = ((), (), s32[]{:S(2)}) async-start(), calls=%async_computation.7 | async-start | bytes 17301504 | tf_op jit(solution)/shard_map/all_gather | solution.py:19
  9.1 78.7 %copy-start.7 = (f32[1024]{0:T(1024)S(1)}, f32[1024]{0:T(1024)}, u32[]{:S(2)}) copy-start(f32[1024]{0:T(1024)} %param.15) | copy-start | bytes 12292
  9.2 181.1 %all-gather.5.cloned.1.call-start = ((), (), s32[]{:S(2)}) async-start(), calls=%async_computation.8 | async-start | bytes 8650752 | tf_op jit(solution)/shard_map/all_gather | solution.py:88
  19.4 20.5 %all-to-all-start.1 = ((s32[64,2,1,2]{3,1,2,0:T(2,128)}), s32[64,2,1,2]{3,1,2,0:T(2,128)S(1)}, u32[]{:S(2)}, u32[]{:S(2)}) async-start(s32[64,2,1,2]{3,1,2,0:T(2,128)} %copy.51), calls=%async_computation.1 | async-start | bytes 131072 | tf_op jit(solution)/shard_map/all_to_all | solution.py:39
  40.1 177.7 %copy-start.6 = (s32[256,1]{0,1:T(1,128)}, s32[256,1]{0,1:T(1,128)S(1)}, u32[]{:S(2)}) copy-start(s32[256,1]{0,1:T(1,128)S(1)} %compare_select_fusion) | copy-start | bytes 3076
  133.5 17.2 %copy-start.2 = (bf16[2,257,1,16,64]{1,4,3,0,2:T(8,128)(2,1)S(1)}, bf16[2,257,1,16,64]{1,4,3,0,2:T(8,128)(2,1)}, u32[]{:S(2)}) copy-start(bf16[2,257,1,16,64]{1,4,3,0,2:T(8,128)(2,1)} %copy.71) | copy-start | bytes 3158020
  160.0 4.1 %copy-start.8 = (f32[1024]{0:T(1024)S(1)}, f32[1024]{0:T(1024)}, u32[]{:S(2)}) copy-start(f32[1024]{0:T(1024)} %param.18) | copy-start | bytes 12292
  190.3 9.1 %copy-start.5 = (f32[1024]{0:T(1024)S(1)}, f32[1024]{0:T(1024)}, u32[]{:S(2)}) copy-start(f32[1024]{0:T(1024)} %param.21) | copy-start | bytes 12292
  204.7 64.5 %copy-start.1 = (f32[1,2048,256]{2,1,0:T(8,128)S(1)}, f32[1,2048,256]{2,1,0:T(8,128)}, u32[]{:S(2)}) copy-start(f32[1,2048,256]{2,1,0:T(8,128)} %param.23) | copy-start | bytes 6291460
  209.7 18.0 %all-to-all-start.3 = ((f32[64,2,1,2,256]{4,3,1,2,0:T(2,128)}), f32[64,2,1,2,256]{4,3,1,2,0:T(2,128)S(1)}, u32[]{:S(2)}, u32[]{:S(2)}) async-start(f32[64,2,1,2,256]{4,3,1,2,0:T(2,128)} %copy.63), calls=%async_computation.3 | async-start | bytes 524288 | tf_op jit(solution)/shard_map/all_to_all | solution.py:39
  220.6 24.9 %copy-start.3 = (pred[64,2,1,2]{3,1,2,0:T(4,128)(4,1)}, pred[64,2,1,2]{3,1,2,0:T(4,128)(4,1)S(1)}, u32[]{:S(2)}) copy-start(pred[64,2,1,2]{3,1,2,0:T(4,128)(4,1)S(1)} %broadcast_compare_fusion) | copy-start | bytes 772
  228.7 16.8 %all-to-all-start.4 = ((f32[128,2,256]{2,1,0:T(2,128)}), f32[128,2,256]{2,1,0:T(2,128)}, u32[]{:S(2)}, u32[]{:S(2)}) async-start(f32[128,2,256]{2,1,0:T(2,128)} %fusion.65), calls=%async_computation.4 | async-start | bytes 524288 | tf_op jit(solution)/shard_map/all_to_all | solution.py:141
  247.6 26.3 %copy-start.4 = (f32[2,256]{1,0:T(2,128)}, f32[2,256]{1,0:T(2,128)S(1)}, u32[]{:S(2)}) copy-start(f32[2,256]{1,0:T(2,128)S(1)} %subtract_multiply_fusion) | copy-start | bytes 6148
  248.4 15.5 %all-to-all-start.6 = ((f32[128,2,256]{2,1,0:T(2,128)}), f32[128,2,256]{2,1,0:T(2,128)S(1)}, u32[]{:S(2)}, u32[]{:S(2)}) async-start(f32[128,2,256]{2,1,0:T(2,128)} %stack.2), calls=%async_computation.6 | async-start | bytes 524288 | tf_op jit(solution)/shard_map/all_to_all | solution.py:156
  263.9 14.8 %all-to-all-start.5 = ((bf16[2,128,8]{2,0,1:T(2,128)(2,1)}), bf16[2,128,8]{2,0,1:T(2,128)(2,1)S(1)}, u32[]{:S(2)}, u32[]{:S(2)}) async-start(bf16[2,128,8]{2,0,1:T(2,128)(2,1)} %copy.66), calls=%async_computation.5 | async-start | bytes 131072 | tf_op jit(solution)/shard_map/all_to_all | solution.py:158
Sparse Core Ops, SparseCore 0:
  10.8 77.0 all-gather.2
  90.1 52.2 all-gather.4
